TPU v7x, 32 devices: a whole 2x2x4 slice. The times are simulated.
32 devices in a mesh: dp: 8 (over z, y), mp: 4 (over x, core).
Axes of the slice: x: 2, y: 2, z: 4, core: 2. Of those that a mesh axis runs over, the one named last changes fastest.
Arguments:
- residual: bfloat16 [16384, 768], P('dp', 'mp'), may hold values from -6 to 6, as said below
- lengths: int32 [8, 4], P('dp'), may hold values from 0 to 2048, as said below
- gain_one: float32 [768], P('mp'), may hold values from 0.5 to 1.5
- input_weight: bfloat16 [3, 768, 768], P(None, None, 'mp'), may hold values from -0.21875 to 0.21875
- input_bias: float32 [2, 768], P(None, 'mp'), may hold values from -1.8 to 1.8
- output_weight: bfloat16 [768, 768], P('mp'), may hold values from -2.5 to 2.5
- output_bias: float32 [768], P('mp'), may hold values from -1.8 to 1.8
- gain_two: float32 [768], P('mp'), may hold values from 0.5 to 1.5
- expand_weight: bfloat16 [768, 3072], P(None, 'mp'), may hold values from -0.21875 to 0.21875
- expand_bias: float32 [3072], P('mp'), may hold values from -1.8 to 1.8
- reduce_weight: bfloat16 [3072, 768], P('mp'), may hold values from -0.109375 to 0.109375
- reduce_bias: float32 [768], P('mp'), may hold values from -1.8 to 1.8
- cotangent: bfloat16 [16384, 768], P('dp', 'mp'), may hold values from -6 to 6
Outputs:
- residual_out: bfloat16 [16384, 768], P('dp', 'mp')
- residual_grad: bfloat16 [16384, 768], P('dp', 'mp')
- input_weight_grad: float32 [3, 768, 768], P(None, None, 'mp')
- input_bias_grad: float32 [2, 768], P(None, 'mp')
- output_weight_grad: float32 [768, 768], P('mp')
- output_bias_grad: float32 [768], P('mp')
- gain_one_grad: float32 [768], P('mp')
- gain_two_grad: float32 [768], P('mp')
- expand_weight_grad: float32 [768, 3072], P(None, 'mp')
- expand_bias_grad: float32 [3072], P('mp')
- reduce_weight_grad: float32 [3072, 768], P('mp')
- reduce_bias_grad: float32 [768], P('mp')
- residual_rms: float32 [], replicated
- live_count: int32 [], replicated
Inputs may be any that keep to these rules, and one draw needn't show every extreme that they name: Each row holds one group's sequence lengths by slot: first some of 2048, then some of 512, then zeros for unused slots; a row sums to at most 2048, and the first row holds a sequence of 2048. `residual`: column 767 is not read.
All inputs are finite; a program needn't handle non-finite values.
Results may differ from a plain program's by a relative error of at most 0.015.
Values may be sent and summed in bfloat16 or wider, within the bound.
A program may use at most 128 MiB of HBM per device.

v0:
```python
import jax
import jax.numpy as jnp
from jax import lax
from jax.sharding import PartitionSpec as P

D = 768
HEAD = 64
SHORT = 512
LONG = 2048
EPSILON = 1e-05
SCORE_SCALE = 0.125
NEGATIVE = -1e30


def smooth(inputs):
    return jax.nn.gelu(inputs, approximate=True)


def layout(width):
    columns = lax.axis_index("mp") * width + jnp.arange(width)
    return (columns < D - 1, columns == D - 1)


def segments(seq_lengths, row_count):
    seq_ends = jnp.cumsum(seq_lengths)
    positions = jnp.arange(row_count)
    segment = jnp.sum((positions[:, None] >= seq_ends[None, :]).astype(jnp.int32), axis=1)
    return (segment, positions < seq_ends[-1])


def window(row_start, row_count, segment, live_rows):
    key_start = jnp.clip(row_start + SHORT - LONG, 0, row_count - LONG)
    query_pos = row_start + jnp.arange(SHORT)
    key_pos = key_start + jnp.arange(LONG)
    query_seg = lax.dynamic_slice_in_dim(segment, row_start, SHORT)
    query_live = lax.dynamic_slice_in_dim(live_rows, row_start, SHORT)
    causal = key_pos[None, :] <= query_pos[:, None]
    allowed = (query_seg[:, None] == segment[None, :]) & causal & query_live[:, None]
    return (key_start, allowed | (key_pos[None, :] == query_pos[:, None]))


def column_sums(values):
    return lax.psum((jnp.sum(values, axis=1), jnp.sum(values * values, axis=1)), "mp")


def gather_normed(normed):
    return lax.all_gather(normed, "mp", axis=1, tiled=True)


def sum_branch(partial_rows, bias_vec):
    return (
        lax.psum_scatter(partial_rows, "mp", scatter_dimension=1, tiled=True) + bias_vec[None, :],
        None,
    )


def spread_grads(grad_rows):
    return lax.all_gather(grad_rows, "mp", axis=1, tiled=True)


def feature_sums(partial_rows):
    return lax.psum_scatter(
        partial_rows.astype(jnp.bfloat16), "mp", scatter_dimension=1, tiled=True
    ).astype(jnp.float32)


def normalize(values, row_total, row_squares, pad_mask, gain_vec):
    decompressed = jnp.where(pad_mask[None, :], -row_total[:, None], values)
    inverse = lax.rsqrt((row_squares + row_total * row_total) / D + EPSILON)
    return (decompressed, inverse, decompressed * inverse[:, None] * gain_vec[None, :])


def add_branch(values, branch, stored):
    kept = stored[None, :]
    row_mean = lax.psum(jnp.sum(branch, axis=1), "mp") / D
    result = values + jnp.where(kept, branch - row_mean[:, None], 0.0)
    new_total, new_squares = column_sums(result)
    return (result, new_total, new_squares)


def attend_forward(queries, key_rows, value_rows, segment, live_rows):
    row_count = queries.shape[0]

    def attend_block(block_index):
        row_start = block_index * SHORT
        key_start, allowed = window(row_start, row_count, segment, live_rows)
        query_block = lax.dynamic_slice_in_dim(queries, row_start, SHORT, 0)
        scores = (
            jnp.einsum("qhd,khd->hqk", query_block, key_rows, preferred_element_type=jnp.float32)
            * SCORE_SCALE
        )
        scores = jnp.where(allowed[None], scores, NEGATIVE)
        row_max = jnp.max(scores, axis=2, keepdims=True)
        weights = jnp.exp(scores - row_max)
        row_sum = jnp.sum(weights, axis=2, keepdims=True)
        attn_probs = (weights / row_sum).astype(jnp.bfloat16)
        result = jnp.einsum(
            "hqk,khd->qhd", attn_probs, value_rows, preferred_element_type=jnp.float32
        )
        return (result.astype(jnp.bfloat16), (row_max + jnp.log(row_sum))[:, :, 0])

    blocks, log_totals = lax.map(attend_block, jnp.arange(row_count // SHORT, dtype=jnp.int32))
    return (blocks.reshape(row_count, queries.shape[1], queries.shape[2]), log_totals)


def attend_backward(queries, key_rows, value_rows, grad_mixed, log_totals, segment, live_rows):
    row_count = queries.shape[0]

    def step(block_index, running):
        grad_queries, grad_keys, grad_values = running
        row_start = block_index * SHORT
        key_start, allowed = window(row_start, row_count, segment, live_rows)
        query_block = lax.dynamic_slice_in_dim(queries, row_start, SHORT, 0)
        grad_block = lax.dynamic_slice_in_dim(grad_mixed, row_start, SHORT, 0)
        scores = (
            jnp.einsum("qhd,khd->hqk", query_block, key_rows, preferred_element_type=jnp.float32)
            * SCORE_SCALE
        )
        scores = jnp.where(allowed[None], scores, NEGATIVE)
        attn_probs = jnp.exp(scores - log_totals[block_index][:, :, None])
        grad_probs = jnp.einsum(
            "qhd,khd->hqk", grad_block, value_rows, preferred_element_type=jnp.float32
        )
        centered = grad_probs - jnp.sum(attn_probs * grad_probs, axis=2, keepdims=True)
        grad_scores = (attn_probs * centered).astype(jnp.bfloat16)
        query_part = (
            jnp.einsum("hqk,khd->qhd", grad_scores, key_rows, preferred_element_type=jnp.float32)
            * SCORE_SCALE
        )
        key_part = (
            jnp.einsum("hqk,qhd->khd", grad_scores, query_block, preferred_element_type=jnp.float32)
            * SCORE_SCALE
        )
        value_part = jnp.einsum(
            "hqk,qhd->khd",
            attn_probs.astype(jnp.bfloat16),
            grad_block,
            preferred_element_type=jnp.float32,
        )
        grad_queries = lax.dynamic_update_slice_in_dim(grad_queries, query_part, row_start, 0)
        grad_keys = grad_keys + key_part
        grad_values = grad_values + value_part
        return (grad_queries, grad_keys, grad_values)

    empty = jnp.zeros(queries.shape, jnp.float32)
    return lax.fori_loop(0, row_count // SHORT, step, (empty, empty, empty))


def on_device(
    residual,
    lengths,
    gain_one,
    input_weight,
    input_bias,
    output_weight,
    output_bias,
    gain_two,
    expand_weight,
    expand_bias,
    reduce_weight,
    reduce_bias,
    cotangent,
):
    row_count, width = residual.shape
    heads_here = width // HEAD
    stored, pad_mask = layout(width)
    segment, live_rows = segments(lengths[0], row_count)
    live_count = lax.psum(jnp.sum(lengths), "dp")
    values = jnp.where(stored[None, :], residual.astype(jnp.float32), 0.0)
    row_total, row_squares = column_sums(values)
    full_one, inverse_one, normed_one = normalize(
        values, row_total, row_squares, pad_mask, gain_one
    )
    rows_one = gather_normed(normed_one.astype(jnp.bfloat16))
    projected = jnp.einsum(
        "td,cde->cte", rows_one, input_weight, preferred_element_type=jnp.float32
    )
    queries = (
        (projected[0] + input_bias[0][None, :])
        .astype(jnp.bfloat16)
        .reshape(row_count, heads_here, HEAD)
    )
    key_rows = projected[1].astype(jnp.bfloat16).reshape(row_count, heads_here, HEAD)
    value_rows = (
        (projected[2] + input_bias[1][None, :])
        .astype(jnp.bfloat16)
        .reshape(row_count, heads_here, HEAD)
    )
    mixed, log_totals = attend_forward(queries, key_rows, value_rows, segment, live_rows)
    mixed = mixed.reshape(row_count, width)
    branch_one, branch_one_total = sum_branch(
        jnp.dot(mixed, output_weight, preferred_element_type=jnp.float32), output_bias
    )
    values_one, total_one, squares_one = add_branch(values, branch_one, stored)
    full_two, inverse_two, normed_two = normalize(
        values_one, total_one, squares_one, pad_mask, gain_two
    )
    rows_two = gather_normed(normed_two.astype(jnp.bfloat16))
    hidden = (
        jnp.dot(rows_two, expand_weight, preferred_element_type=jnp.float32) + expand_bias[None, :]
    )
    active = smooth(hidden).astype(jnp.bfloat16)
    branch_two, branch_two_total = sum_branch(
        jnp.dot(active, reduce_weight, preferred_element_type=jnp.float32), reduce_bias
    )
    values_two, total_two, squares_two = add_branch(values_one, branch_two, stored)
    residual_out = values_two.astype(jnp.bfloat16)
    square_part = jnp.sum(jnp.where(live_rows, squares_two + total_two * total_two, 0.0))
    gradients = jnp.where(stored[None, :], cotangent.astype(jnp.float32), 0.0)
    grad_total = lax.psum(jnp.sum(gradients, axis=1), "mp")
    grad_branch_two = gradients - grad_total[:, None] / D
    reduce_bias_grad = jnp.sum(grad_branch_two, axis=0)
    rows_grad_two = spread_grads(grad_branch_two.astype(jnp.bfloat16))
    reduce_weight_grad = jnp.einsum(
        "tf,td->fd", active, rows_grad_two, preferred_element_type=jnp.float32
    )
    grad_active = jnp.einsum(
        "td,fd->tf", rows_grad_two, reduce_weight, preferred_element_type=jnp.float32
    )
    grad_hidden = jax.vjp(smooth, hidden)[1](grad_active)[0].astype(jnp.bfloat16)
    expand_bias_grad = jnp.sum(grad_hidden, axis=0, dtype=jnp.float32)
    expand_weight_grad = jnp.einsum(
        "td,tf->df", rows_two, grad_hidden, preferred_element_type=jnp.float32
    )
    grad_normed_two = feature_sums(
        jnp.einsum("tf,df->td", grad_hidden, expand_weight, preferred_element_type=jnp.float32)
    )
    gain_two_grad = jnp.sum(grad_normed_two * full_two * inverse_two[:, None], axis=0)
    scaled_two = grad_normed_two * gain_two[None, :]
    projected_two, scaled_total, pad_term = lax.psum(
        (
            jnp.sum(scaled_two * full_two, axis=1),
            jnp.sum(scaled_two, axis=1),
            jnp.sum(jnp.where(pad_mask[None, :], scaled_two, 0.0), axis=1),
        ),
        "mp",
    )
    inverse_cube = inverse_two**3 / D
    grad_full = (
        inverse_two[:, None] * scaled_two - full_two * (inverse_cube * projected_two)[:, None]
    )
    grad_pad = inverse_two * pad_term + total_one * inverse_cube * projected_two
    grad_one = gradients + jnp.where(stored[None, :], grad_full - grad_pad[:, None], 0.0)
    stored_total = grad_total + inverse_two * scaled_total - D * grad_pad
    grad_branch_one = grad_one - stored_total[:, None] / D
    output_bias_grad = jnp.sum(grad_branch_one, axis=0)
    rows_grad_one = spread_grads(grad_branch_one.astype(jnp.bfloat16))
    output_weight_grad = jnp.einsum(
        "tc,td->cd", mixed, rows_grad_one, preferred_element_type=jnp.float32
    )
    grad_mixed = jnp.einsum(
        "td,cd->tc", rows_grad_one, output_weight, preferred_element_type=jnp.float32
    ).astype(jnp.bfloat16)
    query_grads, key_grads, value_grads = attend_backward(
        queries,
        key_rows,
        value_rows,
        grad_mixed.reshape(row_count, heads_here, HEAD),
        log_totals,
        segment,
        live_rows,
    )
    grad_inputs = (
        jnp.stack([query_grads, key_grads, value_grads])
        .astype(jnp.bfloat16)
        .reshape(3, row_count, width)
    )
    input_bias_grad = jnp.stack(
        [
            jnp.sum(grad_inputs[0], axis=0, dtype=jnp.float32),
            jnp.sum(grad_inputs[2], axis=0, dtype=jnp.float32),
        ]
    )
    input_weight_grad = jnp.einsum(
        "td,cte->cde", rows_one, grad_inputs, preferred_element_type=jnp.float32
    )
    grad_normed_one = feature_sums(
        jnp.einsum("cte,cde->td", grad_inputs, input_weight, preferred_element_type=jnp.float32)
    )
    gain_one_grad = jnp.sum(grad_normed_one * full_one * inverse_one[:, None], axis=0)
    scaled_one = grad_normed_one * gain_one[None, :]
    projected_one, pad_first = lax.psum(
        (
            jnp.sum(scaled_one * full_one, axis=1),
            jnp.sum(jnp.where(pad_mask[None, :], scaled_one, 0.0), axis=1),
        ),
        "mp",
    )
    inverse_first = inverse_one**3 / D
    grad_first = (
        inverse_one[:, None] * scaled_one - full_one * (inverse_first * projected_one)[:, None]
    )
    grad_pad_first = inverse_one * pad_first + row_total * inverse_first * projected_one
    residual_grad = (
        grad_one + jnp.where(stored[None, :], grad_first - grad_pad_first[:, None], 0.0)
    ).astype(jnp.bfloat16)
    (
        input_weight_grad,
        input_bias_grad,
        output_weight_grad,
        output_bias_grad,
        gain_one_grad,
        gain_two_grad,
        expand_weight_grad,
        expand_bias_grad,
        reduce_weight_grad,
        reduce_bias_grad,
        square_total,
    ) = lax.psum(
        (
            input_weight_grad,
            input_bias_grad,
            output_weight_grad,
            output_bias_grad,
            gain_one_grad,
            gain_two_grad,
            expand_weight_grad,
            expand_bias_grad,
            reduce_weight_grad,
            reduce_bias_grad,
            square_part,
        ),
        "dp",
    )
    residual_rms = jnp.sqrt(square_total / (D * live_count.astype(jnp.float32)))
    return (
        residual_out,
        residual_grad,
        input_weight_grad,
        input_bias_grad,
        output_weight_grad,
        output_bias_grad,
        gain_one_grad,
        gain_two_grad,
        expand_weight_grad,
        expand_bias_grad,
        reduce_weight_grad,
        reduce_bias_grad,
        residual_rms,
        live_count,
    )


def solution(mesh):
    return jax.shard_map(
        on_device,
        mesh=mesh,
        in_specs=(
            P("dp", "mp"),
            P("dp", None),
            P("mp"),
            P(None, None, "mp"),
            P(None, "mp"),
            P("mp", None),
            P("mp"),
            P("mp"),
            P(None, "mp"),
            P("mp"),
            P("mp", None),
            P("mp"),
            P("dp", "mp"),
        ),
        out_specs=(
            P("dp", "mp"),
            P("dp", "mp"),
            P(None, None, "mp"),
            P(None, "mp"),
            P("mp", None),
            P("mp"),
            P("mp"),
            P("mp"),
            P(None, "mp"),
            P("mp"),
            P("mp", None),
            P("mp"),
            P(),
            P(),
        ),
        check_vma=False,
    )
```

profile of v0, /device:TPU:0, one launch (start us, length us, event | category | flops | bytes accessed | tf_op | source)
XLA Modules:
  0.0 926.3 jit_solution(2679985542805380478)
XLA Ops:
  9.9 12.7 %all-reduce.5 = (f32[2048]{0:T(1024)S(1)}, f32[2048]{0:T(1024)S(1)}) all-reduce(f32[2048]{0:T(1024)S(1)} %get-tuple-element.593, f32[2048]{0:T(1024)S(1)} %get-tuple-element.592), channel_id=1, replica_groups=mesh['dp'=8,'mp'=4] {'mp'}, use_global_device_ids=true, to_apply=%region_5.6 | all-reduce | flops 4096 | bytes 32768 | tf_op jit(solution)/shard_map/psum | solution.py:43
  27.5 27.2 %all-gather.5.cloned.1.call-done = bf16[2048,768]{0,1:T(8,128)(2,1)} async-done(((bf16[2048,192]{0,1:T(8,128)(2,1)}), bf16[2048,768]{0,1:T(8,128)(2,1)}) %all-gather.5.cloned.1.call-update) | async-done | bytes 3145744 | tf_op jit(solution)/shard_map/all_gather | solution.py:47
  59.4 94.8 %while.38 = (s32[]{:T(128)}, bf16[4,512,3,64]{1,3,2,0:T(8,128)(2,1)}, f32[4,3,512]{2,1,0:T(4,128)}, s32[4]{0:T(128)S(1)}, s32[2048]{0:T(1024)S(1)}, /*index=5*/p...) while((s32[]{:T(128)}, ...), condition=%wide.region_9.10_spmd, body=%wide.region_6.9_spmd.sunk | while | flops 849445888 | bytes 43996932 | solution.py:102
  62.4 6.0 fusion.149
  68.4 6.8 fusion.150
  75.2 7.3 fusion.151
  86.1 6.0 fusion.149
  92.1 6.8 fusion.150
  98.9 7.3 fusion.151
  109.8 6.0 fusion.149
  115.8 6.8 fusion.150
  122.6 7.3 fusion.151
  133.5 6.0 fusion.149
  139.5 6.8 fusion.150
  146.2 7.3 fusion.151
  161.1 58.5 %reduce-scatter.5.cloned.1.call-done = f32[2048,192]{0,1:T(8,128)} async-done(((f32[2048,768]{0,1:T(8,128)}), f32[2048,192]{0,1:T(8,128)}) %reduce-scatter.5.cloned.1.call-update) | async-done | bytes 1572880 | tf_op jit(solution)/shard_map/reduce_scatter | solution.py:52
  221.7 6.8 psum.184
  233.5 11.0 %all-reduce.4 = (f32[2048]{0:T(1024)}, f32[2048]{0:T(1024)}, f32[2048]{0:T(1024)}) all-reduce(f32[2048]{0:T(1024)} %get-tuple-element.588, f32[2048]{0:T(1024)} %get-tuple-element.587, f32[2048]{0:T(1024)S(1)} %copy-done.36), channel_id=1, replica_groups=mesh['dp'=8,'mp'=4] {'mp'}, use_global_device_ids=true, to_apply=%region_16.17 | all-reduce | flops 6144 | bytes 49152 | tf_op jit(solution)/shard_map/psum | solution.py:43
  251.6 27.4 %all-gather.7.cloned.1.call-done = bf16[2048,768]{0,1:T(8,128)(2,1)} async-done(((bf16[2048,192]{0,1:T(8,128)(2,1)}), bf16[2048,768]{0,1:T(8,128)(2,1)}) %all-gather.7.cloned.1.call-update) | async-done | bytes 3145744 | tf_op jit(solution)/shard_map/all_gather | solution.py:47
  279.0 7.5 fusion.95
  286.5 23.1 %all-gather.9.cloned.1.call-done = bf16[2048,768]{0,1:T(8,128)(2,1)} async-done(((bf16[2048,192]{0,1:T(8,128)(2,1)}), bf16[2048,768]{0,1:T(8,128)(2,1)}) %all-gather.9.cloned.1.call-update) | async-done | bytes 3145744 | tf_op jit(solution)/shard_map/all_gather | solution.py:58
  309.6 12.7 %convert_reduce_fusion = (f32[768]{0:T(1024)}, bf16[2048,768]{1,0:T(8,128)(2,1)S(1)}, bf16[2048,768]{1,0:T(8,128)(2,1)}) fusion(f32[2048,768]{1,0:T(8,128)} %fusion.95, f32[768]{0:T(1024)} %param.26, bf16[2048,768]{0,1:T(8,128)(2,1)} %all-gather.9.cloned.1.call-done, bf16[768,768]{1,0:T(8,128)(2,1)S(1)} %copy-done), kind=kOutput, calls=%fused_computation.58 | convolution fusion | flops 2455239936 | bytes 16914432 | tf_op jit(solution)/shard_map/td,fd->tf/dot_general | solution.py:217
  328.1 6.5 fusion.96
  334.8 31.4 %reduce-scatter.9.cloned.1.call-done = bf16[2048,192]{0,1:T(8,128)(2,1)} async-done(((bf16[2048,768]{0,1:T(8,128)(2,1)}), bf16[2048,192]{0,1:T(8,128)(2,1)}) %reduce-scatter.9.cloned.1.call-update) | async-done | bytes 786448 | tf_op jit(solution)/shard_map/reduce_scatter | solution.py:62
  369.5 57.5 %reduce-scatter.7.cloned.1.call-done = f32[2048,192]{0,1:T(8,128)} async-done(((f32[2048,768]{0,1:T(8,128)}), f32[2048,192]{0,1:T(8,128)}) %reduce-scatter.7.cloned.1.call-update) | async-done | bytes 1572880 | tf_op jit(solution)/shard_map/reduce_scatter | solution.py:52
  428.6 10.3 %all-reduce.3 = (f32[2048]{0:T(1024)S(1)}, f32[2048]{0:T(1024)S(1)}, f32[2048]{0:T(1024)S(1)}, f32[2048]{0:T(1024)S(1)}) all-reduce(f32[2048]{0:T(1024)S(1)} %add_reduce_fusion, f32[2048]{0:T(1024)S(1)} %get-tuple-element.582, f32[2048]{0:T(1024)S(1)} %get-tuple-element.590, ...), channel_id=1, replica_groups=mesh['dp'=8,'mp'=4] {'mp'}, use_global_device_ids=true, to_apply=%region_19.20 | all-reduce | flops 8192 | bytes 65536 | tf_op jit(solution)/shard_map/psum | solution.py:75
  446.1 29.7 %all-gather.11.cloned.1.call-done = bf16[2048,768]{0,1:T(8,128)(2,1)} async-done(((bf16[2048,192]{0,1:T(8,128)(2,1)}), bf16[2048,768]{0,1:T(8,128)(2,1)}) %all-gather.11.cloned.1.call-update) | async-done | bytes 3145744 | tf_op jit(solution)/shard_map/all_gather | solution.py:58
  479.5 144.6 %while.39 = (s32[]{:T(128)}, bf16[2048,3,64]{0,2,1:T(8,128)(2,1)}, f32[2048,3,64]{0,2,1:T(8,128)}, f32[2048,3,64]{0,2,1:T(8,128)}, s32[2048]{0:T(1024)S(1)}, /*i...) while((s32[]{:T(128)}, bf16[2048,3,64]{0,2,1:T(8,128)(2,1)}, ...), condition=%wide.region_31.32_spmd.clone, body=%wide.region_29.31_spmd.clone.sunk | while | flops 2068808704 | bytes 156712976 | solution.py:146
  500.1 5.8 multiply_reduce_fusion.5
  505.8 6.1 multiply_convert_fusion.5
  511.9 5.8 fusion.162
  527.6 6.1 fusion.164
  533.7 5.8 multiply_reduce_fusion.5
  539.4 6.1 multiply_convert_fusion.5
  545.6 5.8 fusion.162
  561.8 6.1 fusion.164
  567.8 5.8 multiply_reduce_fusion.5
  573.6 6.1 multiply_convert_fusion.5
  579.7 5.8 fusion.162
  595.9 6.1 fusion.164
  607.8 6.1 multiply_convert_fusion.5
  613.9 5.8 fusion.162
  630.6 7.0 fusion.99
  648.2 12.0 %psum.207 = s32[]{:T(128)} all-reduce(s32[]{:T(128)} %reduce_sum.273), channel_id=1, replica_groups=mesh['dp'=8,'mp'=4] {'dp'}, use_global_device_ids=true, to_apply=%region_61.62 | all-reduce | flops 1 | bytes 8 | tf_op jit(solution)/shard_map/psum | solution.py:168
  662.4 6.2 reduce-scatter.11.cloned.1.call-done
  671.0 10.3 %all-reduce.2 = (f32[2048]{0:T(1024)S(1)}, f32[2048]{0:T(1024)S(1)}, f32[2048]{0:T(1024)S(1)}, f32[2048]{0:T(1024)S(1)}) all-reduce(f32[2048]{0:T(1024)S(1)} %get-tuple-element.584, f32[2048]{0:T(1024)S(1)} %get-tuple-element.589, f32[2048]{0:T(1024)S(1)} %copy-done.37, f32[2048]{0:T(1024)S(1)} %copy-done.38), channel_id=1, replica_groups=mesh['dp'=8,'mp'=4] {'mp'}, use_global_device_ids=true, to_apply=%region_34.35 | all-reduce | flops 8192 | bytes 65536 | tf_op jit(solution)/shard_map/psum | solution.py:282
  682.5 39.7 %all-reduce = (f32[2,192]{1,0:T(2,128)}, f32[192]{0:T(256)}, f32[192]{0:T(256)}, f32[192]{0:T(256)}, f32[768]{0:T(1024)}, /*index=5*/f32[192]{0:T(256)}, f32[]{:T(128)}) all-reduce(f32[2,192]{1,0:T(2,128)S(1)} %pad_maximum_fusion.3, f32[192]{0:T(256)S(1)} %copy-done.52, ...), channel_id=1, replica_groups=mesh['dp'=8,'mp'=4] {'dp'}, use_global_device_ids=true, to_apply=%region_40.41 | all-reduce | flops 1921 | bytes 15368 | tf_op jit(solution)/shard_map/psum | solution.py:309
  726.0 184.6 %all-reduce.8.cloned.1.call-done = (f32[3,768,192]{1,2,0:T(8,128)}, f32[192,768]{1,0:T(8,128)}, f32[768,768]{1,0:T(8,128)}, f32[768,768]{1,0:T(8,128)}) async-done(((f32[3,768,192]{1,2,0:T(8,128)}, f32[192,768]{1,0:T(8,128)}, f32[768,768]{1,0:T(8,128)}, f32[768,768]{1,0:T(8,128)}), (f32[3,768,192]{1,2,0:T(8,128)}, f32[192,768]{1,0:T(8,128)}, f32[768,768]{1,0:T(8,128)}, ...) | async-done | bytes 7077904 | tf_op jit(solution)/shard_map/psum | solution.py:309
  (321 shorter events, 150.4 us)
Async XLA Ops:
  7.2 302.5 %copy-start = (bf16[768,768]{1,0:T(8,128)(2,1)S(1)}, bf16[768,768]{1,0:T(8,128)(2,1)}, u32[]{:S(2)}) copy-start(bf16[768,768]{1,0:T(8,128)(2,1)} %param.27) | copy-start | bytes 3538948
  7.2 18.5 %copy-start.63 = (s32[1,4]{1,0:T(1,128)S(1)}, s32[1,4]{1,0:T(1,128)}, u32[]{:S(2)}) copy-start(s32[1,4]{1,0:T(1,128)} %param.18) | copy-start | bytes 52
  7.2 19.3 %copy-start.57 = (f32[2,192]{1,0:T(2,128)S(1)}, f32[2,192]{1,0:T(2,128)}, u32[]{:S(2)}) copy-start(f32[2,192]{1,0:T(2,128)} %param.21) | copy-start | bytes 4612
  7.2 47.5 %copy-start.61 = (bf16[3,768,192]{1,2,0:T(8,128)(2,1)S(1)}, bf16[3,768,192]{1,2,0:T(8,128)(2,1)}, u32[]{:S(2)}) copy-start(bf16[3,768,192]{1,2,0:T(8,128)(2,1)} %param.20) | copy-start | bytes 2654212
  7.2 47.4 %all-gather.5.cloned.1.call-start = ((), (), s32[]{:S(2)}) async-start(), calls=%async_computation.4 | async-start | bytes 3932160 | tf_op jit(solution)/shard_map/all_gather | solution.py:47
  7.3 51.3 %copy-start.43 = (pred[192]{0:T(512)(128)(4,1)}, pred[192]{0:T(512)(128)(4,1)S(1)}, u32[]{:S(2)}) copy-start(pred[192]{0:T(512)(128)(4,1)S(1)} %get-tuple-element.690) | copy-start | bytes 580
  7.3 51.3 %copy-start.46 = (pred[192]{0:T(512)(128)(4,1)}, pred[192]{0:T(512)(128)(4,1)S(1)}, u32[]{:S(2)}) copy-start(pred[192]{0:T(512)(128)(4,1)S(1)} %get-tuple-element.689) | copy-start | bytes 580
  22.6 36.0 %copy-start.41 = (f32[2048]{0:T(1024)}, f32[2048]{0:T(1024)S(1)}, u32[]{:S(2)}) copy-start(f32[2048]{0:T(1024)S(1)} %get-tuple-element.661) | copy-start | bytes 24580
  25.7 193.9 %reduce-scatter.5.cloned.1.call-start = ((), (), s32[]{:S(2)}) async-start(), calls=%async_computation.5 | async-start | bytes 7864320 | tf_op jit(solution)/shard_map/reduce_scatter | solution.py:52
  154.2 6.8 copy-start.56
  161.0 58.5 %copy-start.54 = (f32[192]{0:T(256)S(1)}, f32[192]{0:T(256)}, u32[]{:S(2)}) copy-start(f32[192]{0:T(256)} %param.23) | copy-start | bytes 2308
  161.0 68.2 %copy-start.9 = (bf16[2048,192]{0,1:T(8,128)(2,1)S(1)}, bf16[2048,192]{0,1:T(8,128)(2,1)}, u32[]{:S(2)}) copy-start(bf16[2048,192]{0,1:T(8,128)(2,1)} %param.17) | copy-start | bytes 2359300
  161.0 118.0 %all-gather.7.cloned.1.call-start = ((), (), s32[]{:S(2)}) async-start(), calls=%async_computation.6 | async-start | bytes 3932160 | tf_op jit(solution)/shard_map/all_gather | solution.py:47
  221.7 11.7 %copy-start.36 = (f32[2048]{0:T(1024)S(1)}, f32[2048]{0:T(1024)}, u32[]{:S(2)}) copy-start(f32[2048]{0:T(1024)} %get-tuple-element.597) | copy-start | bytes 24580
  233.4 16.3 %copy-start.14 = (bf16[2048,192]{0,1:T(8,128)(2,1)S(1)}, bf16[2048,192]{0,1:T(8,128)(2,1)}, u32[]{:S(2)}) copy-start(bf16[2048,192]{0,1:T(8,128)(2,1)} %param.29) | copy-start | bytes 2359300
  248.4 61.2 %all-gather.9.cloned.1.call-start = ((), (), s32[]{:S(2)}) async-start(), calls=%async_computation.8 | async-start | bytes 3932160 | tf_op jit(solution)/shard_map/all_gather | solution.py:58
  251.6 114.6 %reduce-scatter.9.cloned.1.call-start = ((), (), s32[]{:S(2)}) async-start(), calls=%async_computation.9 | async-start | bytes 3932160 | tf_op jit(solution)/shard_map/reduce_scatter | solution.py:62
  309.6 14.4 %copy-start.60 = (bf16[768,768]{1,0:T(8,128)(2,1)S(1)}, bf16[768,768]{1,0:T(8,128)(2,1)}, u32[]{:S(2)}) copy-start(bf16[768,768]{1,0:T(8,128)(2,1)} %param.25) | copy-start | bytes 3538948
  328.1 98.9 %reduce-scatter.7.cloned.1.call-start = ((), (), s32[]{:S(2)}) async-start(), calls=%async_computation.7 | async-start | bytes 7864320 | tf_op jit(solution)/shard_map/reduce_scatter | solution.py:52
  334.6 31.5 %copy-start.33 = (f32[2048]{0:T(1024)S(1)}, f32[2048]{0:T(1024)}, u32[]{:S(2)}) copy-start(f32[2048]{0:T(1024)} %copy-done.32) | copy-start | bytes 24580
  334.6 31.5 %copy-start.47 = (pred[192]{0:T(512)(128)(4,1)S(1)}, pred[192]{0:T(512)(128)(4,1)}, u32[]{:S(2)}) copy-start(pred[192]{0:T(512)(128)(4,1)} %copy-done.46) | copy-start | bytes 580
  334.6 31.5 %copy-start.49 = (f32[192]{0:T(256)S(1)}, f32[192]{0:T(256)}, u32[]{:S(2)}) copy-start(f32[192]{0:T(256)} %param.24) | copy-start | bytes 2308
  334.7 92.3 %copy-start.55 = (f32[192]{0:T(256)S(1)}, f32[192]{0:T(256)}, u32[]{:S(2)}) copy-start(f32[192]{0:T(256)} %param.28) | copy-start | bytes 2308
  334.7 104.2 %copy-start.39 = (f32[2048]{0:T(1024)S(1)}, f32[2048]{0:T(1024)}, u32[]{:S(2)}) copy-start(f32[2048]{0:T(1024)} %get-tuple-element.659) | copy-start | bytes 24580
  334.7 104.2 %copy-start.40 = (f32[2048]{0:T(1024)S(1)}, f32[2048]{0:T(1024)}, u32[]{:S(2)}) copy-start(f32[2048]{0:T(1024)} %get-tuple-element.658) | copy-start | bytes 24580
  334.7 104.2 %copy-start.44 = (pred[192]{0:T(512)(128)(4,1)S(1)}, pred[192]{0:T(512)(128)(4,1)}, u32[]{:S(2)}) copy-start(pred[192]{0:T(512)(128)(4,1)} %copy-done.43) | copy-start | bytes 580
  334.7 141.1 %all-gather.11.cloned.1.call-start = ((), (), s32[]{:S(2)}) async-start(), calls=%async_computation.10 | async-start | bytes 3932160 | tf_op jit(solution)/shard_map/all_gather | solution.py:58
  366.2 72.8 %copy-start.21 = (bf16[2048,192]{0,1:T(8,128)(2,1)S(1)}, bf16[2048,192]{0,1:T(8,128)(2,1)}, u32[]{:S(2)}) copy-start(bf16[2048,192]{0,1:T(8,128)(2,1)} %reduce-scatter.9.cloned.1.call-done) | copy-start | bytes 2359300
  443.8 32.0 %copy-start.26 = (bf16[192,768]{1,0:T(8,128)(2,1)S(1)}, bf16[192,768]{1,0:T(8,128)(2,1)}, u32[]{:S(2)}) copy-start(bf16[192,768]{1,0:T(8,128)(2,1)} %param.22) | copy-start | bytes 884740
  446.1 222.5 %reduce-scatter.11.cloned.1.call-start = ((), (), s32[]{:S(2)}) async-start(), calls=%async_computation.11 | async-start | bytes 3932160 | tf_op jit(solution)/shard_map/reduce_scatter | solution.py:62
  630.5 280.1 %all-reduce.8.cloned.1.call-start = ((), (), s32[]{:S(2)}) async-start(), calls=%async_computation.12 | async-start | bytes 14155776 | tf_op jit(solution)/shard_map/psum | solution.py:309
  630.5 7.1 copy-start.59
  630.6 7.1 copy-start.66
  646.9 21.7 %copy-start.10 = (bf16[2048,192]{0,1:T(8,128)(2,1)S(1)}, bf16[2048,192]{0,1:T(8,128)(2,1)}, u32[]{:S(2)}) copy-start(bf16[2048,192]{0,1:T(8,128)(2,1)} %param.17) | copy-start | bytes 2359300
  646.9 21.7 %copy-start.15 = (bf16[2048,192]{0,1:T(8,128)(2,1)S(1)}, bf16[2048,192]{0,1:T(8,128)(2,1)}, u32[]{:S(2)}) copy-start(bf16[2048,192]{0,1:T(8,128)(2,1)} %param.29) | copy-start | bytes 2359300
  646.9 21.7 %copy-start.29 = (f32[2048]{0:T(1024)S(1)}, f32[2048]{0:T(1024)}, u32[]{:S(2)}) copy-start(f32[2048]{0:T(1024)} %copy-done.28) | copy-start | bytes 24580
  646.9 21.7 %copy-start.31 = (f32[2048]{0:T(1024)S(1)}, f32[2048]{0:T(1024)}, u32[]{:S(2)}) copy-start(f32[2048]{0:T(1024)} %copy-done.30) | copy-start | bytes 24580
  646.9 21.7 %copy-start.35 = (f32[2048]{0:T(1024)S(1)}, f32[2048]{0:T(1024)}, u32[]{:S(2)}) copy-start(f32[2048]{0:T(1024)} %copy-done.34) | copy-start | bytes 24580
  646.9 21.7 %copy-start.45 = (pred[192]{0:T(512)(128)(4,1)S(1)}, pred[192]{0:T(512)(128)(4,1)}, u32[]{:S(2)}) copy-start(pred[192]{0:T(512)(128)(4,1)} %copy-done.43) | copy-start | bytes 580
  646.9 21.7 %copy-start.48 = (pred[192]{0:T(512)(128)(4,1)S(1)}, pred[192]{0:T(512)(128)(4,1)}, u32[]{:S(2)}) copy-start(pred[192]{0:T(512)(128)(4,1)} %copy-done.46) | copy-start | bytes 580
  646.9 21.7 %copy-start.50 = (f32[192]{0:T(256)S(1)}, f32[192]{0:T(256)}, u32[]{:S(2)}) copy-start(f32[192]{0:T(256)} %param.19) | copy-start | bytes 2308
  647.6 23.4 %copy-start.37 = (f32[2048]{0:T(1024)S(1)}, f32[2048]{0:T(1024)}, u32[]{:S(2)}) copy-start(f32[2048]{0:T(1024)} %get-tuple-element.679) | copy-start | bytes 24580
  647.6 23.4 %copy-start.38 = (f32[2048]{0:T(1024)S(1)}, f32[2048]{0:T(1024)}, u32[]{:S(2)}) copy-start(f32[2048]{0:T(1024)} %get-tuple-element.680) | copy-start | bytes 24580
  647.6 35.0 %copy-start.51 = (f32[192]{0:T(256)S(1)}, f32[192]{0:T(256)}, u32[]{:S(2)}) copy-start(f32[192]{0:T(256)} %get-tuple-element.581) | copy-start | bytes 2308
  647.6 35.0 %copy-start.52 = (f32[192]{0:T(256)S(1)}, f32[192]{0:T(256)}, u32[]{:S(2)}) copy-start(f32[192]{0:T(256)} %get-tuple-element.664) | copy-start | bytes 2308
  647.6 35.0 %copy-start.53 = (f32[768]{0:T(1024)S(1)}, f32[768]{0:T(1024)}, u32[]{:S(2)}) copy-start(f32[768]{0:T(1024)} %get-tuple-element.662) | copy-start | bytes 9220
  647.6 75.4 %copy-start.42 = (f32[2048]{0:T(1024)S(1)}, f32[2048]{0:T(1024)}, u32[]{:S(2)}) copy-start(f32[2048]{0:T(1024)} %copy-done.41) | copy-start | bytes 24580
  647.6 75.4 %copy-start.12 = (f32[2048,192]{0,1:T(8,128)S(1)}, f32[2048,192]{0,1:T(8,128)}, u32[]{:S(2)}) copy-start(f32[2048,192]{0,1:T(8,128)} %copy-done.11) | copy-start | bytes 4718596
  (52 other events, 204.2 us)
Sparse Core Ops, SparseCore 0:
  25.8 28.8 all-gather.4
  161.2 58.3 reduce-scatter.4
  248.5 30.4 all-gather.6
  281.1 28.5 all-gather.8
  328.2 37.9 reduce-scatter.8
  368.6 58.3 reduce-scatter.6
  446.2 29.5 all-gather.10
  630.6 37.9 reduce-scatter.10
  674.2 236.3 all-reduce.7
where the time goes:
time: 936 us; the launch traced here: 926 us
  waiting for transfers between devices  446 us (48%)
  matrix products  212 us (23%)
  other arithmetic  107 us (11%)
  blocking collectives  103 us (11%)
  local copies, waits for them, and re-layouts  28.5 us (3%)
  between operations  17.3 us (2%)
  loops' own time  13 us (1%)
    psum x1, waiting for transfers between devices, on_device(): lax.psum((input_weight_grad, input_bias_grad, output_weight_grad, output_...  185 us
    reduce_scatter x2, waiting for transfers between devices, sum_branch(): lax.psum_scatter(partial_rows, 'mp', scatter_dimension=1, tiled=True)  116 us
    all_gather x2, waiting for transfers between devices, gather_normed(): return lax.all_gather(normed, 'mp', axis=1, tiled=True)  54.6 us
    all_gather x2, waiting for transfers between devices, spread_grads(): return lax.all_gather(grad_rows, 'mp', axis=1, tiled=True)  52.8 us
    psum x1, blocking collectives, on_device(): lax.psum((input_weight_grad, input_bias_grad, output_weight_grad, output_...  39.7 us
    reduce_scatter x2, waiting for transfers between devices, feature_sums(): lax.psum_scatter(partial_rows.astype(jnp.bfloat16), 'mp', scatter_dimensi...  37.6 us
    dot_general x4, matrix products, attend_block(): jnp.einsum('hqk,khd->qhd', attn_probs, value_rows, preferred_element_type...  29.3 us
    reduce_sum x4, other arithmetic, attend_block(): row_sum = jnp.sum(weights, axis=2, keepdims=True)  27.1 us
  transfers between devices with their start and end apart: 9, of which 9 were waited for; matrix products, arithmetic and copies ran while one was open for 5% of the time, Pallas kernels for 0%

commit v1 on v0

--- a/solution.py
+++ b/solution.py
@@ -10,6 +10,27 @@
 EPSILON = 1e-05
 SCORE_SCALE = 0.125
 NEGATIVE = -1e30
+
+
+def gather_around(x, axis, dim):
+    count, index, extent = (lax.axis_size(axis), lax.axis_index(axis), x.shape[dim])
+    forward = [(i, (i + 1) % count) for i in range(count)]
+    backward = [(i, (i - 1) % count) for i in range(count)]
+    out = jnp.zeros((*x.shape[:dim], count * extent, *x.shape[dim + 1 :]), x.dtype)
+    out = lax.dynamic_update_slice_in_dim(out, x, index * extent, axis=dim)
+    from_left = from_right = x
+    half = count // 2
+    for step in range(1, half + 1):
+        from_left = lax.ppermute(from_left, axis, forward)
+        out = lax.dynamic_update_slice_in_dim(
+            out, from_left, (index - step) % count * extent, axis=dim
+        )
+        if step < count - half:
+            from_right = lax.ppermute(from_right, axis, backward)
+            out = lax.dynamic_update_slice_in_dim(
+                out, from_right, (index + step) % count * extent, axis=dim
+            )
+    return out
 
 
 def smooth(inputs):
@@ -44,7 +65,7 @@
 
 
 def gather_normed(normed):
-    return lax.all_gather(normed, "mp", axis=1, tiled=True)
+    return gather_around(normed, "mp", 1)
 
 
 def sum_branch(partial_rows, bias_vec):

time: 936 us -> 998 us (1.066)
  local copies, waits for them, and re-layouts: 28.5 us -> 131 us
  waiting for transfers between devices: 446 us -> 410 us
  starting transfers between devices: 0.37 us -> 11 us
    dynamic_update_slice x0 -> x8, local copies, waits for them, and re-layouts: none -> 86.2 us  [the longest x4 42.2 us: gather_around(): lax.dynamic_update_slice_in_dim(out, from_left, (index - step) % count *...]
    all_gather x2 -> x0, waiting for transfers between devices: 54.6 us -> none  [gather_normed(): return lax.all_gather(normed, 'mp', axis=1, tiled=True)]
    ppermute x0 -> x6, waiting for transfers between devices: none -> 39.9 us  [the longest x4 39.9 us: gather_around(): from_left = lax.ppermute(from_left, axis, forward)]
    all_gather x2, waiting for transfers between devices: 52.8 us -> 29.7 us  [spread_grads(): return lax.all_gather(grad_rows, 'mp', axis=1, tiled=True)]
    ppermute x0 -> x6, local copies, waits for them, and re-layouts: none -> 10.9 us  [the longest x4 7.29 us: gather_around(): from_left = lax.ppermute(from_left, axis, forward)]
    ppermute x0 -> x6, starting transfers between devices: none -> 10.3 us  [the longest x4 7.49 us: gather_around(): from_left = lax.ppermute(from_left, axis, forward)]
  transfers between devices with their start and end apart: 9 -> 13, of which waited for: 9 -> 8; matrix products, arithmetic and copies ran while one was open for 5% -> 13% of each run, Pallas kernels for 0% -> 0%
where the time goes in v1:
time: 998 us; the launch traced here: 984 us
  waiting for transfers between devices  410 us (41%)
  matrix products  205 us (21%)
  local copies, waits for them, and re-layouts  131 us (13%)
  other arithmetic  104 us (10%)
  blocking collectives  102 us (10%)
  between operations  17.8 us (2%)
  starting transfers between devices  11 us (1%)
    psum x1, waiting for transfers between devices, on_device(): lax.psum((input_weight_grad, input_bias_grad, output_weight_grad, output_...  185 us
    reduce_scatter x2, waiting for transfers between devices, sum_branch(): lax.psum_scatter(partial_rows, 'mp', scatter_dimension=1, tiled=True)  117 us
    dynamic_update_slice x4, local copies, waits for them, and re-layouts, gather_around(): lax.dynamic_update_slice_in_dim(out, from_left, (index - step) % count *...  42.2 us
    ppermute x4, waiting for transfers between devices, gather_around(): from_left = lax.ppermute(from_left, axis, forward)  39.9 us
    psum x1, blocking collectives, on_device(): lax.psum((input_weight_grad, input_bias_grad, output_weight_grad, output_...  39.7 us
    reduce_scatter x2, waiting for transfers between devices, feature_sums(): lax.psum_scatter(partial_rows.astype(jnp.bfloat16), 'mp', scatter_dimensi...  38.8 us
    all_gather x2, waiting for transfers between devices, spread_grads(): return lax.all_gather(grad_rows, 'mp', axis=1, tiled=True)  29.7 us
    dot_general x4, matrix products, attend_block(): jnp.einsum('hqk,khd->qhd', attn_probs, value_rows, preferred_element_type...  29.3 us
  transfers between devices with their start and end apart: 13, of which 8 were waited for; matrix products, arithmetic and copies ran while one was open for 13% of the time, Pallas kernels for 0%

profile of v1, /device:TPU:0, one launch (start us, length us, event | category | flops | bytes accessed | tf_op | source)
XLA Modules:
  0.0 984.5 jit_solution(6832550262938993240)
XLA Ops:
  9.9 12.7 %all-reduce.5 = (f32[2048]{0:T(1024)S(1)}, f32[2048]{0:T(1024)S(1)}) all-reduce(f32[2048]{0:T(1024)S(1)} %get-tuple-element.593, f32[2048]{0:T(1024)S(1)} %get-tuple-element.592), channel_id=1, replica_groups=mesh['dp'=8,'mp'=4] {'mp'}, use_global_device_ids=true, to_apply=%region_5.6 | all-reduce | flops 4096 | bytes 32768 | tf_op jit(solution)/shard_map/psum | solution.py:64
  25.9 17.5 %collective-permute-done = bf16[2048,192]{0,1:T(8,128)(2,1)} collective-permute-done((bf16[2048,192]{0,1:T(8,128)(2,1)S(1)}, bf16[2048,192]{0,1:T(8,128)(2,1)}, u32[]{:S(2)}, u32[]{:S(2)}) %collective-permute-start) | collective-permute-done | bytes 786464 | tf_op jit(solution)/shard_map/ppermute | solution.py:24
  46.9 10.2 %dynamic_update_slice.57 = bf16[2048,768]{1,0:T(8,128)(2,1)} dynamic-update-slice(bf16[2048,768]{1,0:T(8,128)(2,1)} %broadcast.387.clone, bf16[2048,192]{1,0:T(8,128)(2,1)S(1)} %copy.44, s32[]{:T(128)} %constant.254.clone.1, s32[]{:T(128)S(6)} %select_n.135) | dynamic-update-slice | bytes 1572868 | tf_op jit(solution)/shard_map/dynamic_update_slice | solution.py:20
  59.2 10.7 %dynamic_update_slice.58 = bf16[2048,768]{1,0:T(8,128)(2,1)} dynamic-update-slice(bf16[2048,768]{1,0:T(8,128)(2,1)} %dynamic_update_slice.57, bf16[2048,192]{1,0:T(8,128)(2,1)S(1)} %copy.45, s32[]{:T(128)} %constant.254.clone.1, s32[]{:T(128)S(6)} %select_n.137) | dynamic-update-slice | bytes 1572868 | tf_op jit(solution)/shard_map/dynamic_update_slice | solution.py:25
  71.3 11.4 %dynamic_update_slice.59 = bf16[2048,768]{1,0:T(8,128)(2,1)} dynamic-update-slice(bf16[2048,768]{1,0:T(8,128)(2,1)} %dynamic_update_slice.58, bf16[2048,192]{1,0:T(8,128)(2,1)S(1)} %copy.46, s32[]{:T(128)} %constant.254.clone.1, s32[]{:T(128)S(6)} %select_n.139) | dynamic-update-slice | bytes 1572868 | tf_op jit(solution)/shard_map/dynamic_update_slice | solution.py:30
  84.2 9.9 %dynamic_update_slice.60 = bf16[2048,768]{1,0:T(8,128)(2,1)} dynamic-update-slice(bf16[2048,768]{1,0:T(8,128)(2,1)} %dynamic_update_slice.59, bf16[2048,192]{1,0:T(8,128)(2,1)S(1)} %copy.47, s32[]{:T(128)} %constant.254.clone.1, s32[]{:T(128)S(6)} %select_n.141) | dynamic-update-slice | bytes 1572868 | tf_op jit(solution)/shard_map/dynamic_update_slice | solution.py:25
  99.0 94.8 %while.38 = (s32[]{:T(128)}, bf16[4,512,3,64]{1,3,2,0:T(8,128)(2,1)}, f32[4,3,512]{2,1,0:T(4,128)}, s32[4]{0:T(128)S(1)}, s32[2048]{0:T(1024)S(1)}, /*index=5*/p...) while((s32[]{:T(128)}, ...), condition=%wide.region_9.10_spmd, body=%wide.region_6.9_spmd.sunk | while | flops 849445888 | bytes 43996932 | solution.py:123
  102.1 6.0 fusion.149
  108.0 6.8 fusion.150
  114.8 7.3 fusion.151
  125.7 6.0 fusion.149
  131.7 6.8 fusion.150
  138.5 7.3 fusion.151
  149.4 6.0 fusion.149
  155.4 6.8 fusion.150
  162.2 7.3 fusion.151
  173.1 6.0 fusion.149
  179.1 6.8 fusion.150
  185.9 7.3 fusion.151
  201.0 59.5 %reduce-scatter.5.cloned.1.call-done = f32[2048,192]{0,1:T(8,128)} async-done(((f32[2048,768]{0,1:T(8,128)}), f32[2048,192]{0,1:T(8,128)}) %reduce-scatter.5.cloned.1.call-update) | async-done | bytes 1572880 | tf_op jit(solution)/shard_map/reduce_scatter | solution.py:73
  262.8 6.5 psum.184
  274.2 10.3 %all-reduce.4 = (f32[2048]{0:T(1024)S(1)}, f32[2048]{0:T(1024)S(1)}, f32[2048]{0:T(1024)S(1)}) all-reduce(f32[2048]{0:T(1024)} %get-tuple-element.588, f32[2048]{0:T(1024)} %get-tuple-element.587, f32[2048]{0:T(1024)S(1)} %copy-done.38), channel_id=1, replica_groups=mesh['dp'=8,'mp'=4] {'mp'}, use_global_device_ids=true, to_apply=%region_16.17 | all-reduce | flops 6144 | bytes 49152 | tf_op jit(solution)/shard_map/psum | solution.py:64
  290.5 22.4 %collective-permute-done.3 = bf16[2048,192]{0,1:T(8,128)(2,1)} collective-permute-done((bf16[2048,192]{0,1:T(8,128)(2,1)S(1)}, bf16[2048,192]{0,1:T(8,128)(2,1)}, u32[]{:S(2)}, u32[]{:S(2)}) %collective-permute-start.3) | collective-permute-done | bytes 786464 | tf_op jit(solution)/shard_map/ppermute | solution.py:24
  312.9 6.7 collective-permute-start.5
  322.7 10.5 %dynamic_update_slice.61 = bf16[2048,768]{1,0:T(8,128)(2,1)} dynamic-update-slice(bf16[2048,768]{1,0:T(8,128)(2,1)} %broadcast.387, bf16[2048,192]{1,0:T(8,128)(2,1)} %copy.49, s32[]{:T(128)} %constant.254.clone.1, s32[]{:T(128)S(6)} %select_n.135) | dynamic-update-slice | bytes 1572868 | tf_op jit(solution)/shard_map/dynamic_update_slice | solution.py:20
  335.5 11.2 %dynamic_update_slice.62 = bf16[2048,768]{1,0:T(8,128)(2,1)} dynamic-update-slice(bf16[2048,768]{1,0:T(8,128)(2,1)} %dynamic_update_slice.61, bf16[2048,192]{1,0:T(8,128)(2,1)} %copy.50, s32[]{:T(128)} %constant.254.clone.1, s32[]{:T(128)S(6)} %select_n.137) | dynamic-update-slice | bytes 1572868 | tf_op jit(solution)/shard_map/dynamic_update_slice | solution.py:25
  348.9 11.9 %dynamic_update_slice.63 = bf16[2048,768]{1,0:T(8,128)(2,1)} dynamic-update-slice(bf16[2048,768]{1,0:T(8,128)(2,1)} %dynamic_update_slice.62, bf16[2048,192]{1,0:T(8,128)(2,1)} %copy.51, s32[]{:T(128)} %constant.254.clone.1, s32[]{:T(128)S(6)} %select_n.139) | dynamic-update-slice | bytes 1572868 | tf_op jit(solution)/shard_map/dynamic_update_slice | solution.py:30
  363.0 10.4 %dynamic_update_slice.64 = bf16[2048,768]{1,0:T(8,128)(2,1)} dynamic-update-slice(bf16[2048,768]{1,0:T(8,128)(2,1)} %dynamic_update_slice.63, bf16[2048,192]{1,0:T(8,128)(2,1)} %copy.52, s32[]{:T(128)} %constant.254.clone.1, s32[]{:T(128)S(6)} %select_n.141) | dynamic-update-slice | bytes 1572868 | tf_op jit(solution)/shard_map/dynamic_update_slice | solution.py:25
  378.6 8.6 convert_reduce_fusion
  394.1 6.5 fusion.96
  400.8 32.7 %reduce-scatter.9.cloned.1.call-done = bf16[2048,192]{0,1:T(8,128)(2,1)} async-done(((bf16[2048,768]{0,1:T(8,128)(2,1)}), bf16[2048,192]{0,1:T(8,128)(2,1)}) %reduce-scatter.9.cloned.1.call-update) | async-done | bytes 786448 | tf_op jit(solution)/shard_map/reduce_scatter | solution.py:83
  436.8 57.5 %reduce-scatter.7.cloned.1.call-done = f32[2048,192]{0,1:T(8,128)} async-done(((f32[2048,768]{0,1:T(8,128)}), f32[2048,192]{0,1:T(8,128)}) %reduce-scatter.7.cloned.1.call-update) | async-done | bytes 1572880 | tf_op jit(solution)/shard_map/reduce_scatter | solution.py:73
  495.9 10.3 %all-reduce.3 = (f32[2048]{0:T(1024)S(1)}, f32[2048]{0:T(1024)S(1)}, f32[2048]{0:T(1024)S(1)}, f32[2048]{0:T(1024)S(1)}) all-reduce(f32[2048]{0:T(1024)S(1)} %add_reduce_fusion, f32[2048]{0:T(1024)S(1)} %get-tuple-element.582, f32[2048]{0:T(1024)S(1)} %get-tuple-element.590, ...), channel_id=1, replica_groups=mesh['dp'=8,'mp'=4] {'mp'}, use_global_device_ids=true, to_apply=%region_19.20 | all-reduce | flops 8192 | bytes 65536 | tf_op jit(solution)/shard_map/psum | solution.py:96
  513.4 29.7 %all-gather.5.cloned.1.call-done = bf16[2048,768]{0,1:T(8,128)(2,1)} async-done(((bf16[2048,192]{0,1:T(8,128)(2,1)}), bf16[2048,768]{0,1:T(8,128)(2,1)}) %all-gather.5.cloned.1.call-update) | async-done | bytes 3145744 | tf_op jit(solution)/shard_map/all_gather | solution.py:79
  546.8 135.1 %while.39 = (s32[]{:T(128)}, bf16[2048,3,64]{0,2,1:T(8,128)(2,1)}, f32[2048,3,64]{0,2,1:T(8,128)}, f32[2048,3,64]{0,2,1:T(8,128)}, s32[2048]{0:T(1024)S(1)}, /*i...) while((s32[]{:T(128)}, bf16[2048,3,64]{0,2,1:T(8,128)(2,1)}, ...), condition=%wide.region_31.32_spmd.clone, body=%wide.region_29.31_spmd.clone.sunk | while | flops 2068808704 | bytes 156712976 | solution.py:167
  563.6 6.1 multiply_convert_fusion.5
  585.4 6.1 fusion.164
  597.2 6.1 multiply_convert_fusion.5
  619.6 6.1 fusion.164
  631.4 6.1 multiply_convert_fusion.5
  653.7 6.1 fusion.164
  665.6 6.1 multiply_convert_fusion.5
  688.4 7.1 fusion.99
  706.1 12.0 %psum.207 = s32[]{:T(128)} all-reduce(s32[]{:T(128)} %reduce_sum.273), channel_id=1, replica_groups=mesh['dp'=8,'mp'=4] {'dp'}, use_global_device_ids=true, to_apply=%region_61.62 | all-reduce | flops 1 | bytes 8 | tf_op jit(solution)/shard_map/psum | solution.py:189
  720.3 6.1 reduce-scatter.11.cloned.1.call-done
  728.8 10.3 %all-reduce.2 = (f32[2048]{0:T(1024)S(1)}, f32[2048]{0:T(1024)S(1)}, f32[2048]{0:T(1024)S(1)}, f32[2048]{0:T(1024)S(1)}) all-reduce(f32[2048]{0:T(1024)S(1)} %get-tuple-element.584, f32[2048]{0:T(1024)S(1)} %get-tuple-element.589, f32[2048]{0:T(1024)S(1)} %copy-done.39, f32[2048]{0:T(1024)S(1)} %copy-done.40), channel_id=1, replica_groups=mesh['dp'=8,'mp'=4] {'mp'}, use_global_device_ids=true, to_apply=%region_34.35 | all-reduce | flops 8192 | bytes 65536 | tf_op jit(solution)/shard_map/psum | solution.py:303
  740.3 39.7 %all-reduce = (f32[2,192]{1,0:T(2,128)}, f32[192]{0:T(256)}, f32[192]{0:T(256)}, f32[192]{0:T(256)}, f32[768]{0:T(1024)}, /*index=5*/f32[192]{0:T(256)}, f32[]{:T(128)}) all-reduce(f32[2,192]{1,0:T(2,128)S(1)} %pad_maximum_fusion.3, f32[192]{0:T(256)S(1)} %copy-done.56, ...), channel_id=1, replica_groups=mesh['dp'=8,'mp'=4] {'dp'}, use_global_device_ids=true, to_apply=%region_40.41 | all-reduce | flops 1921 | bytes 15368 | tf_op jit(solution)/shard_map/psum | solution.py:330
  783.7 184.7 %all-reduce.8.cloned.1.call-done = (f32[3,768,192]{1,2,0:T(8,128)}, f32[192,768]{1,0:T(8,128)}, f32[768,768]{1,0:T(8,128)}, f32[768,768]{1,0:T(8,128)}) async-done(((f32[3,768,192]{1,2,0:T(8,128)}, f32[192,768]{1,0:T(8,128)}, f32[768,768]{1,0:T(8,128)}, f32[768,768]{1,0:T(8,128)}), (f32[3,768,192]{1,2,0:T(8,128)}, f32[192,768]{1,0:T(8,128)}, f32[768,768]{1,0:T(8,128)}, ...) | async-done | bytes 7077904 | tf_op jit(solution)/shard_map/psum | solution.py:330
  (351 shorter events, 213.3 us)
Async XLA Ops:
  7.2 371.4 %copy-start = (bf16[768,768]{1,0:T(8,128)(2,1)S(1)}, bf16[768,768]{1,0:T(8,128)(2,1)}, u32[]{:S(2)}) copy-start(bf16[768,768]{1,0:T(8,128)(2,1)} %param.25) | copy-start | bytes 3538948
  7.2 253.4 %reduce-scatter.5.cloned.1.call-start = ((), (), s32[]{:S(2)}) async-start(), calls=%async_computation.4 | async-start | bytes 7864320 | tf_op jit(solution)/shard_map/reduce_scatter | solution.py:73
  7.3 36.2 %copy-start.47 = (pred[192]{0:T(512)(128)(4,1)}, pred[192]{0:T(512)(128)(4,1)S(1)}, u32[]{:S(2)}) copy-start(pred[192]{0:T(512)(128)(4,1)S(1)} %get-tuple-element.690) | copy-start | bytes 580
  7.3 36.2 %copy-start.50 = (pred[192]{0:T(512)(128)(4,1)}, pred[192]{0:T(512)(128)(4,1)S(1)}, u32[]{:S(2)}) copy-start(pred[192]{0:T(512)(128)(4,1)S(1)} %get-tuple-element.689) | copy-start | bytes 580
  7.3 36.7 %copy-start.66 = (s32[1,4]{1,0:T(1,128)S(1)}, s32[1,4]{1,0:T(1,128)}, u32[]{:S(2)}) copy-start(s32[1,4]{1,0:T(1,128)} %param.18) | copy-start | bytes 52
  7.3 37.5 %copy-start.61 = (f32[2,192]{1,0:T(2,128)S(1)}, f32[2,192]{1,0:T(2,128)}, u32[]{:S(2)}) copy-start(f32[2,192]{1,0:T(2,128)} %param.21) | copy-start | bytes 4612
  22.5 20.9 %copy-start.45 = (f32[2048]{0:T(1024)}, f32[2048]{0:T(1024)S(1)}, u32[]{:S(2)}) copy-start(f32[2048]{0:T(1024)S(1)} %get-tuple-element.661) | copy-start | bytes 24580
  22.6 20.9 %copy-start.32 = (f32[2048]{0:T(1024)}, f32[2048]{0:T(1024)S(1)}, u32[]{:S(2)}) copy-start(f32[2048]{0:T(1024)S(1)} %get-tuple-element.687) | copy-start | bytes 24580
  24.1 19.3 %collective-permute-start = (bf16[2048,192]{0,1:T(8,128)(2,1)S(1)}, bf16[2048,192]{0,1:T(8,128)(2,1)}, u32[]{:S(2)}, u32[]{:S(2)}) collective-permute-start(bf16[2048,192]{0,1:T(8,128)(2,1)S(1)} %multiply_convert_fusion.3), channel_id=1, source_target_pairs={{0,1},{1,2},{2,3},{3,0},{4,5},{5,6},{6,7},{7,4},{8,9},{9,10},{10,1... | collective-permute-start | bytes 2359304 | tf_op jit(solution)/shard_map/ppermute | solution.py:24
  24.2 45.7 %collective-permute-start.1 = (bf16[2048,192]{0,1:T(8,128)(2,1)S(1)}, bf16[2048,192]{0,1:T(8,128)(2,1)}, u32[]{:S(2)}, u32[]{:S(2)}) collective-permute-start(bf16[2048,192]{0,1:T(8,128)(2,1)S(1)} %multiply_convert_fusion.3), channel_id=1, source_target_pairs={{0,3},{1,0},{2,1},{3,2},{4,7},{5,4},{6,5},{7,6},{8,11},{9,8},{10,9... | collective-permute-start | bytes 2359304 | tf_op jit(solution)/shard_map/ppermute | solution.py:29
  43.4 39.3 %collective-permute-start.2 = (bf16[2048,192]{0,1:T(8,128)(2,1)}, bf16[2048,192]{0,1:T(8,128)(2,1)}, u32[]{:S(2)}, u32[]{:S(2)}) collective-permute-start(bf16[2048,192]{0,1:T(8,128)(2,1)} %collective-permute-done), channel_id=1, source_target_pairs={{0,1},{1,2},{2,3},{3,0},{4,5},{5,6},{6,7},{7,4},{8,9},{9,10},{10,1... | collective-permute-start | bytes 2359304 | tf_op jit(solution)/shard_map/ppermute | solution.py:24
  200.6 60.0 %copy-start.58 = (f32[192]{0:T(256)S(1)}, f32[192]{0:T(256)}, u32[]{:S(2)}) copy-start(f32[192]{0:T(256)} %param.23) | copy-start | bytes 2308
  200.6 69.4 %copy-start.9 = (bf16[2048,192]{0,1:T(8,128)(2,1)S(1)}, bf16[2048,192]{0,1:T(8,128)(2,1)}, u32[]{:S(2)}) copy-start(bf16[2048,192]{0,1:T(8,128)(2,1)} %param.17) | copy-start | bytes 2359300
  200.6 172.8 %all-gather.3.cloned.1.call-start = ((), (), s32[]{:S(2)}) async-start(), calls=%async_computation.6 | async-start | bytes 3932160 | tf_op jit(solution)/shard_map/all_gather | solution.py:79
  286.9 146.6 %reduce-scatter.9.cloned.1.call-start = ((), (), s32[]{:S(2)}) async-start(), calls=%async_computation.7 | async-start | bytes 3932160 | tf_op jit(solution)/shard_map/reduce_scatter | solution.py:83
  286.9 25.9 %copy-start.34 = (f32[2048]{0:T(1024)}, f32[2048]{0:T(1024)S(1)}, u32[]{:S(2)}) copy-start(f32[2048]{0:T(1024)S(1)} %get-tuple-element.685) | copy-start | bytes 24580
  288.7 24.2 %collective-permute-start.3 = (bf16[2048,192]{0,1:T(8,128)(2,1)S(1)}, bf16[2048,192]{0,1:T(8,128)(2,1)}, u32[]{:S(2)}, u32[]{:S(2)}) collective-permute-start(bf16[2048,192]{0,1:T(8,128)(2,1)S(1)} %multiply_convert_fusion.2), channel_id=1, source_target_pairs={{0,1},{1,2},{2,3},{3,0},{4,5},{5,6},{6,7},{7,4},{8,9},{9,10},{10,1... | collective-permute-start | bytes 2359304 | tf_op jit(solution)/shard_map/ppermute | solution.py:24
  289.4 57.3 %collective-permute-start.4 = (bf16[2048,192]{0,1:T(8,128)(2,1)S(1)}, bf16[2048,192]{0,1:T(8,128)(2,1)}, u32[]{:S(2)}, u32[]{:S(2)}) collective-permute-start(bf16[2048,192]{0,1:T(8,128)(2,1)S(1)} %multiply_convert_fusion.2), channel_id=1, source_target_pairs={{0,3},{1,0},{2,1},{3,2},{4,7},{5,4},{6,5},{7,6},{8,11},{9,8},{10,9... | collective-permute-start | bytes 2359304 | tf_op jit(solution)/shard_map/ppermute | solution.py:29
  312.9 48.0 %collective-permute-start.5 = (bf16[2048,192]{0,1:T(8,128)(2,1)}, bf16[2048,192]{0,1:T(8,128)(2,1)}, u32[]{:S(2)}, u32[]{:S(2)}) collective-permute-start(bf16[2048,192]{0,1:T(8,128)(2,1)} %collective-permute-done.3), channel_id=1, source_target_pairs={{0,1},{1,2},{2,3},{3,0},{4,5},{5,6},{6,7},{7,4},{8,9},{9,10},{10,1... | collective-permute-start | bytes 2359304 | tf_op jit(solution)/shard_map/ppermute | solution.py:24
  392.9 101.4 %reduce-scatter.7.cloned.1.call-start = ((), (), s32[]{:S(2)}) async-start(), calls=%async_computation.5 | async-start | bytes 7864320 | tf_op jit(solution)/shard_map/reduce_scatter | solution.py:73
  400.6 32.8 %copy-start.35 = (f32[2048]{0:T(1024)S(1)}, f32[2048]{0:T(1024)}, u32[]{:S(2)}) copy-start(f32[2048]{0:T(1024)} %copy-done.34) | copy-start | bytes 24580
  400.6 32.8 %copy-start.51 = (pred[192]{0:T(512)(128)(4,1)S(1)}, pred[192]{0:T(512)(128)(4,1)}, u32[]{:S(2)}) copy-start(pred[192]{0:T(512)(128)(4,1)} %copy-done.50) | copy-start | bytes 580
  400.6 32.8 %copy-start.53 = (f32[192]{0:T(256)S(1)}, f32[192]{0:T(256)}, u32[]{:S(2)}) copy-start(f32[192]{0:T(256)} %param.24) | copy-start | bytes 2308
  400.7 93.6 %copy-start.59 = (f32[192]{0:T(256)S(1)}, f32[192]{0:T(256)}, u32[]{:S(2)}) copy-start(f32[192]{0:T(256)} %param.28) | copy-start | bytes 2308
  400.7 105.5 %copy-start.42 = (f32[2048]{0:T(1024)S(1)}, f32[2048]{0:T(1024)}, u32[]{:S(2)}) copy-start(f32[2048]{0:T(1024)} %copy-done.41) | copy-start | bytes 24580
  400.7 105.5 %copy-start.44 = (f32[2048]{0:T(1024)S(1)}, f32[2048]{0:T(1024)}, u32[]{:S(2)}) copy-start(f32[2048]{0:T(1024)} %copy-done.43) | copy-start | bytes 24580
  400.7 105.5 %copy-start.14 = (bf16[2048,192]{0,1:T(8,128)(2,1)S(1)}, bf16[2048,192]{0,1:T(8,128)(2,1)}, u32[]{:S(2)}) copy-start(bf16[2048,192]{0,1:T(8,128)(2,1)} %param.29) | copy-start | bytes 2359300
  400.7 105.5 %copy-start.48 = (pred[192]{0:T(512)(128)(4,1)S(1)}, pred[192]{0:T(512)(128)(4,1)}, u32[]{:S(2)}) copy-start(pred[192]{0:T(512)(128)(4,1)} %copy-done.47) | copy-start | bytes 580
  400.7 142.4 %all-gather.5.cloned.1.call-start = ((), (), s32[]{:S(2)}) async-start(), calls=%async_computation.8 | async-start | bytes 3932160 | tf_op jit(solution)/shard_map/all_gather | solution.py:79
  433.5 72.8 %copy-start.21 = (bf16[2048,192]{0,1:T(8,128)(2,1)S(1)}, bf16[2048,192]{0,1:T(8,128)(2,1)}, u32[]{:S(2)}) copy-start(bf16[2048,192]{0,1:T(8,128)(2,1)} %reduce-scatter.9.cloned.1.call-done) | copy-start | bytes 2359300
  511.1 32.0 %copy-start.28 = (bf16[192,768]{1,0:T(8,128)(2,1)S(1)}, bf16[192,768]{1,0:T(8,128)(2,1)}, u32[]{:S(2)}) copy-start(bf16[192,768]{1,0:T(8,128)(2,1)} %param.22) | copy-start | bytes 884740
  513.4 213.0 %reduce-scatter.11.cloned.1.call-start = ((), (), s32[]{:S(2)}) async-start(), calls=%async_computation.9 | async-start | bytes 3932160 | tf_op jit(solution)/shard_map/reduce_scatter | solution.py:83
  688.3 280.1 %all-reduce.8.cloned.1.call-start = ((), (), s32[]{:S(2)}) async-start(), calls=%async_computation.10 | async-start | bytes 14155776 | tf_op jit(solution)/shard_map/psum | solution.py:330
  704.8 21.6 %copy-start.10 = (bf16[2048,192]{0,1:T(8,128)(2,1)S(1)}, bf16[2048,192]{0,1:T(8,128)(2,1)}, u32[]{:S(2)}) copy-start(bf16[2048,192]{0,1:T(8,128)(2,1)} %param.17) | copy-start | bytes 2359300
  704.8 21.6 %copy-start.15 = (bf16[2048,192]{0,1:T(8,128)(2,1)S(1)}, bf16[2048,192]{0,1:T(8,128)(2,1)}, u32[]{:S(2)}) copy-start(bf16[2048,192]{0,1:T(8,128)(2,1)} %param.29) | copy-start | bytes 2359300
  704.8 21.6 %copy-start.31 = (f32[2048]{0:T(1024)S(1)}, f32[2048]{0:T(1024)}, u32[]{:S(2)}) copy-start(f32[2048]{0:T(1024)} %copy-done.30) | copy-start | bytes 24580
  704.8 21.6 %copy-start.33 = (f32[2048]{0:T(1024)S(1)}, f32[2048]{0:T(1024)}, u32[]{:S(2)}) copy-start(f32[2048]{0:T(1024)} %copy-done.32) | copy-start | bytes 24580
  704.8 21.6 %copy-start.37 = (f32[2048]{0:T(1024)S(1)}, f32[2048]{0:T(1024)}, u32[]{:S(2)}) copy-start(f32[2048]{0:T(1024)} %copy-done.36) | copy-start | bytes 24580
  704.8 21.6 %copy-start.49 = (pred[192]{0:T(512)(128)(4,1)S(1)}, pred[192]{0:T(512)(128)(4,1)}, u32[]{:S(2)}) copy-start(pred[192]{0:T(512)(128)(4,1)} %copy-done.47) | copy-start | bytes 580
  704.8 21.6 %copy-start.52 = (pred[192]{0:T(512)(128)(4,1)S(1)}, pred[192]{0:T(512)(128)(4,1)}, u32[]{:S(2)}) copy-start(pred[192]{0:T(512)(128)(4,1)} %copy-done.50) | copy-start | bytes 580
  704.8 21.6 %copy-start.54 = (f32[192]{0:T(256)S(1)}, f32[192]{0:T(256)}, u32[]{:S(2)}) copy-start(f32[192]{0:T(256)} %param.19) | copy-start | bytes 2308
  705.4 23.3 %copy-start.39 = (f32[2048]{0:T(1024)S(1)}, f32[2048]{0:T(1024)}, u32[]{:S(2)}) copy-start(f32[2048]{0:T(1024)} %get-tuple-element.679) | copy-start | bytes 24580
  705.4 23.3 %copy-start.40 = (f32[2048]{0:T(1024)S(1)}, f32[2048]{0:T(1024)}, u32[]{:S(2)}) copy-start(f32[2048]{0:T(1024)} %get-tuple-element.680) | copy-start | bytes 24580
  705.4 34.9 %copy-start.55 = (f32[192]{0:T(256)S(1)}, f32[192]{0:T(256)}, u32[]{:S(2)}) copy-start(f32[192]{0:T(256)} %get-tuple-element.581) | copy-start | bytes 2308
  705.4 34.9 %copy-start.56 = (f32[192]{0:T(256)S(1)}, f32[192]{0:T(256)}, u32[]{:S(2)}) copy-start(f32[192]{0:T(256)} %get-tuple-element.664) | copy-start | bytes 2308
  705.4 34.9 %copy-start.57 = (f32[768]{0:T(1024)S(1)}, f32[768]{0:T(1024)}, u32[]{:S(2)}) copy-start(f32[768]{0:T(1024)} %get-tuple-element.662) | copy-start | bytes 9220
  705.4 75.3 %copy-start.46 = (f32[2048]{0:T(1024)S(1)}, f32[2048]{0:T(1024)}, u32[]{:S(2)}) copy-start(f32[2048]{0:T(1024)} %copy-done.45) | copy-start | bytes 24580
  705.4 75.3 %copy-start.12 = (f32[2048,192]{0,1:T(8,128)S(1)}, f32[2048,192]{0,1:T(8,128)}, u32[]{:S(2)}) copy-start(f32[2048,192]{0,1:T(8,128)} %copy-done.11) | copy-start | bytes 4718596
  (59 other events, 274.0 us)
Sparse Core Ops, SparseCore 0:
  200.8 59.7 reduce-scatter.4
  287.0 43.9 all-gather.2
  393.0 40.4 reduce-scatter.8
  435.8 58.3 reduce-scatter.6
  513.5 29.5 all-gather.4
  688.4 37.9 reduce-scatter.10
  732.0 236.4 all-reduce.7
